TPU v7x, 128 devices: a whole 4x4x4 slice. The times are simulated.
128 devices in a mesh: heads: 4 (over z), ctx: 32 (over y, x, core).
Axes of the slice: x: 4, y: 4, z: 4, core: 2. Of those that a mesh axis runs over, the one named last changes fastest.
Arguments:
- queries: bfloat16 [16384, 2048], P('ctx', 'heads'), may hold values from -6 to 6
- key_heads: bfloat16 [16384, 1024], P('ctx', 'heads'), may hold values from -6 to 6
- value_heads: bfloat16 [16384, 1024], P('ctx', 'heads'), may hold values from -6 to 6
- class_ids: int32 [16384], P('ctx'), may hold values from 0 to 63
- level_table: float32 [64, 16, 9], P(None, 'heads'), may hold values from 0.25 to 2
- out_weight: bfloat16 [2048, 2048], P('ctx', 'heads'), may hold values from -0.125 to 0.125
- out_grad: bfloat16 [16384, 2048], P('ctx', 'heads'), may hold values from -6 to 6
Outputs:
- projected: bfloat16 [16384, 2048], P('ctx', 'heads')
- query_grad: bfloat16 [16384, 2048], P('ctx', 'heads')
- key_grad: bfloat16 [16384, 1024], P('ctx', 'heads')
- value_grad: bfloat16 [16384, 1024], P('ctx', 'heads')
- weight_grad: float32 [2048, 2048], P('ctx', 'heads')
All inputs are finite; a program needn't handle non-finite values.
Results may differ from a plain program's by a relative error of at most 0.017.
Values may be sent and summed in bfloat16 or wider, within the bound.
A program may use at most 128 MiB of HBM per device.

v0:
```python
import jax
import jax.numpy as jnp
from jax import lax
from jax.experimental import pallas as pl
from jax.experimental.pallas import tpu as pltpu
from jax.sharding import PartitionSpec as P

DH = 128
CH = 64
RING = 4
LOCAL = 4
CROSS = 5
TILE = 256
TOKENS = 512
WIDTH = 512
HEADS = 4
GROUPS = 2
BF16 = jnp.bfloat16
F32 = jnp.float32


def coefficient(level):
    return DH ** (-0.5) * (CH * 2 ** max(level - 1, 0)) ** (-0.5)


def contract(a, b, da, db, precision=None):
    return lax.dot_general(
        a, b, (((da,), (db,)), ((), ())), preferred_element_type=F32, precision=precision
    )


def dot(a, b):
    return contract(a, b, 1, 0)


def dot_nt(a, b):
    return contract(a, b, 1, 1)


def dot_tn(a, b):
    return contract(a, b, 0, 0)


def ring(index, offset):
    return lax.rem(index + offset + RING, RING)


def flag(condition):
    return condition.astype(jnp.int32).astype(F32)


def make_kernel(norm):
    def kernel(
        q_ref, k_ref, v_ref, ids_ref, tab_ref, w_ref, og_ref,
        proj_ref, dq_ref, dk_ref, dv_ref, wg_ref,
        ogf, wf, acc, attn, ga, piece, zbuf, wg, wgc, ybuf, xpiece, xbuf,
        scale, wqc, prob, total, ssend, srecv, read, gmat, gacc, gsend, grecv, dka, dva,
        ssem, rsem,
    ):
        z = lax.axis_index("heads")
        c = lax.axis_index("ctx")
        core = lax.rem(c, 2)
        x = lax.rem(c // 2, RING)
        y = c // 8
        used = [0]
        sent = []

        def z_dev(offset):
            return {"heads": ring(z, offset)}

        def x_dev(offset):
            return {"ctx": (y * RING + ring(x, offset)) * 2 + core}

        def y_dev(offset):
            return {"ctx": (ring(y, offset) * RING + x) * 2 + core}

        sibling = {"ctx": (y * RING + x) * 2 + 1 - core}

        def send(src, dst, device):
            number = used[0]
            used[0] = number + 1
            copy = pltpu.make_async_remote_copy(
                src_ref=src,
                dst_ref=dst,
                send_sem=ssem.at[number],
                recv_sem=rsem.at[number],
                device_id=device,
                device_id_type=pl.DeviceIdType.MESH,
            )
            copy.start()
            sent.append(copy)
            return copy

        def gather_start(dev, index, half):
            right, left = dev(1), dev(-1)
            a = send(half(index, 0), half(index, 0), right)
            b = send(half(index, 1), half(index, 1), left)
            d = send(half(index, 1), half(index, 1), right)
            e = send(half(index, 0), half(index, 0), left)
            return a, b, d, e

        def gather_forward(dev, index, half, copies):
            before, after = ring(index, -1), ring(index, 1)
            copies[0].wait_recv()
            a = send(half(before, 0), half(before, 0), dev(1))
            copies[1].wait_recv()
            b = send(half(after, 1), half(after, 1), dev(-1))
            return a, b

        def scatter_far(dev, index, half, buf):
            far = ring(index, 2)
            return (
                send(half(far, 0), buf.at[0], dev(1)),
                send(half(far, 1), buf.at[3], dev(-1)),
            )

        def scatter_near(dev, index, half, buf):
            return (
                send(half(ring(index, 1), 1), buf.at[1], dev(1)),
                send(half(ring(index, -1), 0), buf.at[4], dev(-1)),
            )

        def scatter_middle(dev, index, half, buf, far):
            after, before = half(ring(index, 1), 0), half(ring(index, -1), 1)
            far[0].wait_recv()
            after[...] = (after[...].astype(F32) + buf[0].astype(F32)).astype(BF16)
            a = send(after, buf.at[2], dev(1))
            far[1].wait_recv()
            before[...] = (before[...].astype(F32) + buf[3].astype(F32)).astype(BF16)
            b = send(before, buf.at[5], dev(-1))
            return a, b

        def scatter_wait(near, middle):
            for copy in near + middle:
                copy.wait_recv()

        def scatter_sum(index, half, buf, part):
            own = half(index, part)[...].astype(F32)
            if part == 0:
                return own + buf[2].astype(F32) + buf[4].astype(F32)
            return own + buf[1].astype(F32) + buf[5].astype(F32)

        barrier = pltpu.get_barrier_semaphore()
        peers = [z_dev(1), z_dev(-1), sibling]
        for offset in (1, 2, 3):
            peers += [x_dev(offset), y_dev(offset)]
        for device in peers:
            pl.semaphore_signal(
                barrier, inc=1, device_id=device, device_id_type=pl.DeviceIdType.MESH
            )
        pl.semaphore_wait(barrier, len(peers))

        def og_half(block, part):
            return ogf.at[block, pl.ds(part * TILE, TILE)]

        ogf[z] = og_ref[...]
        og_copies = gather_start(z_dev, z, og_half)

        own = y * RING + x
        wf[own, core] = w_ref[...]
        w_x = [send(wf.at[own, core], wf.at[own, core], x_dev(o)) for o in (1, 3, 2)]

        for g in range(GROUPS):
            cols = slice(g * DH, (g + 1) * DH)
            total[g] = dot_tn(k_ref[:, cols], v_ref[:, cols])
        ssend[0] = total[...].astype(BF16)
        s_core = send(ssend.at[0], srecv.at[0], sibling)

        classes = tab_ref.shape[0]
        onehot = (
            lax.broadcasted_iota(jnp.int32, (classes, TOKENS), 0) == ids_ref[...]
        ).astype(F32)
        levels = LOCAL + CROSS
        level = lax.broadcasted_iota(jnp.int32, (1, levels), 1)
        coef = jnp.full((1, levels), coefficient(0), F32)
        for number in range(1, levels):
            coef = jnp.where(level == number, coefficient(number), coef)
        for h in range(HEADS):
            lam = contract(onehot, tab_ref[:, h, :], 0, 0, lax.Precision.HIGHEST)
            scale[h] = lam * coef

        def w_half(block, part):
            return wf.at[pl.ds(block * RING + part * 2, 2), core]

        def w_row(block):
            return wf.at[pl.ds(block * RING, RING), core]

        for copy in w_x:
            copy.wait_recv()
        w_y = gather_start(y_dev, y, w_half)
        w_rows = [send(w_row(y), w_row(y), sibling)]

        s_core.wait_recv()
        got = srecv[0].astype(F32)
        for g in range(GROUPS):
            read[g, 0:DH] = (got[g] * flag(core == 1)).astype(BF16)
        total[...] += got
        ssend[1] = total[...].astype(BF16)
        s_x = [send(ssend.at[1], srecv.at[o], x_dev(o)) for o in (1, 2, 3)]

        def weigh(h):
            cols = pl.ds(pl.multiple_of(h * DH, DH), DH)
            q = q_ref[:, cols].astype(F32)
            for l in range(CROSS):
                wqc[h, :, l * DH : (l + 1) * DH] = (
                    q * scale[h, :, LOCAL + l : LOCAL + l + 1]
                ).astype(BF16)

        lax.fori_loop(0, HEADS, lambda h, _: (weigh(h), 0)[1], 0)

        og_far = gather_forward(z_dev, z, og_half, og_copies)

        def exchange(copies, position, slot, low):
            near = jnp.zeros((GROUPS, DH, DH), F32)
            far = jnp.zeros((GROUPS, DH, DH), F32)
            everything = total[...]
            for o, copy in zip((1, 2, 3), copies):
                copy.wait_recv()
                source = ring(position, -o)
                value = srecv[slot + o].astype(F32)
                upper = source < position
                same = source // 2 == position // 2
                near += value * flag(jnp.logical_and(upper, same))
                far += value * flag(jnp.logical_and(upper, jnp.logical_not(same)))
                everything += value
            for g in range(GROUPS):
                read[g, low * DH : (low + 1) * DH] = near[g].astype(BF16)
                read[g, (low + 1) * DH : (low + 2) * DH] = far[g].astype(BF16)
            total[...] = everything

        exchange(s_x, x, 0, 1)
        ssend[2] = total[...].astype(BF16)
        s_y = [send(ssend.at[2], srecv.at[3 + o], y_dev(o)) for o in (1, 2, 3)]

        rows = lax.broadcasted_iota(jnp.int32, (TILE, TILE), 0)
        cols_ = lax.broadcasted_iota(jnp.int32, (TILE, TILE), 1)

        def tile_weight(h, i):
            span = pl.ds(i * TILE, TILE)
            weight = jnp.where(
                rows // (2 * CH) > cols_ // (2 * CH), scale[h, span, 2:3], 0.0
            )
            weight = jnp.where(
                jnp.logical_and(
                    rows // (2 * CH) == cols_ // (2 * CH), rows // CH > cols_ // CH
                ),
                scale[h, span, 1:2],
                weight,
            )
            return jnp.where(
                jnp.logical_and(rows // CH == cols_ // CH, rows >= cols_),
                scale[h, span, 0:1],
                weight,
            )

        first, second = pl.ds(0, TILE), pl.ds(TILE, TILE)

        def forward(h):
            cols = pl.ds(pl.multiple_of(h * DH, DH), DH)
            group = pl.ds(pl.multiple_of(h // 2 * DH, DH), DH)
            q0, q1 = q_ref[first, cols], q_ref[second, cols]
            k0, k1 = k_ref[first, group], k_ref[second, group]
            v0, v1 = v_ref[first, group], v_ref[second, group]
            p0 = (dot_nt(q0, k0) * tile_weight(h, 0)).astype(BF16)
            p1 = (dot_nt(q1, k1) * tile_weight(h, 1)).astype(BF16)
            p2 = (dot_nt(q1, k0) * scale[h, second, 3:4]).astype(BF16)
            prob[h, 0] = p0
            prob[h, 1] = p1
            prob[h, 2] = p2
            acc[first, cols] = dot(p0, v0)
            acc[second, cols] = dot(p1, v1) + dot(p2, v0)

        lax.fori_loop(0, 2, lambda h, _: (forward(h), 0)[1], 0)
        w_far = gather_forward(y_dev, y, w_half, w_y)
        lax.fori_loop(2, HEADS, lambda h, _: (forward(h), 0)[1], 0)
        w_y[2].wait_recv()
        w_rows.append(send(w_row(ring(y, -1)), w_row(ring(y, -1)), sibling))
        w_y[3].wait_recv()
        w_rows.append(send(w_row(ring(y, 1)), w_row(ring(y, 1)), sibling))
        exchange(s_y, y, 3, 3)

        def across(h):
            cols = pl.ds(pl.multiple_of(h * DH, DH), DH)
            attn[:, cols] = (acc[:, cols] + dot(wqc[h], read[h // 2])).astype(BF16)

        lax.fori_loop(0, HEADS, lambda h, _: (across(h), 0)[1], 0)
        w_far[0].wait_recv()
        w_far[1].wait_recv()
        w_rows.append(send(w_row(ring(y, 2)), w_row(ring(y, 2)), sibling))
        for copy in w_rows:
            copy.wait_recv()

        def weights(block):
            return wf[pl.ds(block * RING, RING)].reshape(WIDTH, WIDTH)

        def project(block):
            def step(t, _):
                span = pl.ds(pl.multiple_of(t * TILE, TILE), TILE)
                piece[block, span] = dot_nt(attn[span], weights(block)).astype(BF16)
                return 0

            lax.fori_loop(0, 2, step, 0)

        def z_half(block, part):
            return piece.at[block, pl.ds(part * TILE, TILE)]

        project(ring(z, 2))
        z_far = scatter_far(z_dev, z, z_half, zbuf)
        project(ring(z, 1))
        project(ring(z, -1))
        z_near = scatter_near(z_dev, z, z_half, zbuf)

        def back(block, start):
            def step(t, _):
                span = pl.ds(pl.multiple_of(t * TILE, TILE), TILE)
                term = dot(ogf[block, span], weights(block))
                acc[span] = term if start else acc[span] + term
                return 0

            lax.fori_loop(0, 2, step, 0)

        wg_core = []

        def weight_grad(block):
            def step(t, _):
                span = pl.ds(pl.multiple_of(t * TILE, TILE), TILE)
                term = dot_tn(ogf[block, :, span], attn[...]).astype(BF16)
                wg[pl.ds(block * RING + t * 2, 2)] = term.reshape(2, 2, CH, WIDTH)
                return 0

            lax.fori_loop(0, 2, step, 0)
            span = pl.ds(block * RING, RING)
            wg_core.append(send(wg.at[span, 1 - core], wgc.at[span], sibling))

        back(z, True)
        weight_grad(z)
        project(z)
        og_copies[2].wait_recv()
        back(ring(z, -1), False)
        og_copies[3].wait_recv()
        back(ring(z, 1), False)
        weight_grad(ring(z, -1))
        weight_grad(ring(z, 1))
        og_far[0].wait_recv()
        og_far[1].wait_recv()
        back(ring(z, 2), False)
        ga[...] = acc[...].astype(BF16)
        z_middle = scatter_middle(z_dev, z, z_half, zbuf, z_far)
        weight_grad(ring(z, 2))

        def state_grad(g):
            value = jnp.zeros((DH, CROSS * DH), F32)
            for r in range(2):
                h = g * 2 + r
                cols = pl.ds(pl.multiple_of(h * DH, DH), DH)
                value += dot_tn(ga[:, cols], wqc[h])
            gmat[g] = value

        lax.fori_loop(0, GROUPS, lambda g, _: (state_grad(g), 0)[1], 0)

        def level_grad(number):
            return gmat[:, :, number * DH : (number + 1) * DH]

        g_y = []
        for o in (1, 2, 3):
            same = flag(y // 2 == ring(y, o) // 2)
            gsend[o] = (level_grad(3) * same + level_grad(4) * (1.0 - same)).astype(BF16)
            g_y.append(send(gsend.at[o], grecv.at[o], y_dev(o)))

        for copy in wg_core:
            copy.wait_recv()

        def merge(t, _):
            wgc[t] = (wg[t, core].astype(F32) + wgc[t].astype(F32)).astype(BF16)
            return 0

        lax.fori_loop(0, RING * RING, merge, 0)

        def y_half(block, part):
            return wgc.at[pl.ds(block * RING + part * 2, 2)]

        y_far = scatter_far(y_dev, y, y_half, ybuf)
        y_near = scatter_near(y_dev, y, y_half, ybuf)

        def backward(g):
            group = pl.ds(pl.multiple_of(g * DH, DH), DH)
            k0, k1 = k_ref[first, group], k_ref[second, group]
            v0, v1 = v_ref[first, group], v_ref[second, group]
            for r in range(2):
                h = g * 2 + r
                cols = pl.ds(pl.multiple_of(h * DH, DH), DH)
                q0, q1 = q_ref[first, cols], q_ref[second, cols]
                g0, g1 = ga[first, cols], ga[second, cols]
                d0 = (dot_nt(g0, v0) * tile_weight(h, 0)).astype(BF16)
                d1 = (dot_nt(g1, v1) * tile_weight(h, 1)).astype(BF16)
                d2 = (dot_nt(g1, v0) * scale[h, second, 3:4]).astype(BF16)
                dq0 = dot(d0, k0)
                dq1 = dot(d1, k1) + dot(d2, k0)
                y0, y1 = dot_nt(g0, read[g]), dot_nt(g1, read[g])
                for l in range(CROSS):
                    part = slice(l * DH, (l + 1) * DH)
                    number = slice(LOCAL + l, LOCAL + l + 1)
                    dq0 += y0[:, part] * scale[h, first, number]
                    dq1 += y1[:, part] * scale[h, second, number]
                dq_ref[first, cols] = dq0.astype(BF16)
                dq_ref[second, cols] = dq1.astype(BF16)
                p0, p1, p2 = prob[h, 0], prob[h, 1], prob[h, 2]
                dk0 = dot_tn(d0, q0) + dot_tn(d2, q1)
                dk1 = dot_tn(d1, q1)
                dv0 = dot_tn(p0, g0) + dot_tn(p2, g1)
                dv1 = dot_tn(p1, g1)
                if r == 0:
                    dka[first, group] = dk0
                    dka[second, group] = dk1
                    dva[first, group] = dv0
                    dva[second, group] = dv1
                else:
                    dka[first, group] += dk0
                    dka[second, group] += dk1
                    dva[first, group] += dv0
                    dva[second, group] += dv1

        backward_loop = lambda a, b: lax.fori_loop(a, b, lambda g, _: (backward(g), 0)[1], 0)
        backward_loop(0, 1)

        y_middle = scatter_middle(y_dev, y, y_half, ybuf, y_far)
        gacc[...] = jnp.zeros_like(gacc)
        for o, copy in zip((1, 2, 3), g_y):
            copy.wait_recv()
            gacc[...] += grecv[o].astype(F32) * flag(ring(y, -o) > y)
        g_x = []
        for o in (1, 2, 3):
            same = flag(x // 2 == ring(x, o) // 2)
            lower = flag(x > ring(x, o))
            gsend[3 + o] = (
                gacc[...]
                + level_grad(1) * (lower * same)
                + level_grad(2) * (lower * (1.0 - same))
            ).astype(BF16)
            g_x.append(send(gsend.at[3 + o], grecv.at[3 + o], x_dev(o)))
        backward_loop(1, 2)
        for o, copy in zip((1, 2, 3), g_x):
            copy.wait_recv()
            gacc[...] += grecv[3 + o].astype(F32)
        gsend[0] = (gacc[...] + level_grad(0) * flag(core == 1)).astype(BF16)
        g_core = send(gsend.at[0], grecv.at[0], sibling)

        scatter_wait(y_near, y_middle)
        xpiece[0:2] = scatter_sum(y, y_half, ybuf, 0).astype(BF16)
        xpiece[2:4] = scatter_sum(y, y_half, ybuf, 1).astype(BF16)

        def x_half(block, part):
            return xpiece.at[block, pl.ds(part * 32, 32)]

        x_far = scatter_far(x_dev, x, x_half, xbuf)
        x_near = scatter_near(x_dev, x, x_half, xbuf)

        g_core.wait_recv()
        gacc[...] += grecv[0].astype(F32)
        for g in range(GROUPS):
            cols = slice(g * DH, (g + 1) * DH)
            key_side = gacc[g].astype(BF16)
            dk_ref[:, cols] = (dka[:, cols] + dot(v_ref[:, cols], key_side)).astype(BF16)
            dv_ref[:, cols] = (dva[:, cols] + dot_nt(k_ref[:, cols], key_side)).astype(BF16)

        x_middle = scatter_middle(x_dev, x, x_half, xbuf, x_far)
        scatter_wait(x_near, x_middle)
        wg_ref[0:32] = scatter_sum(x, x_half, xbuf, 0) * norm
        wg_ref[32:64] = scatter_sum(x, x_half, xbuf, 1) * norm

        scatter_wait(z_near, z_middle)
        proj_ref[0:TILE] = scatter_sum(z, z_half, zbuf, 0).astype(BF16)
        proj_ref[TILE:] = scatter_sum(z, z_half, zbuf, 1).astype(BF16)
        for copy in sent:
            copy.wait_send()

    return kernel


COPIES = 60


def local(queries, key_heads, value_heads, class_ids, level_table, out_weight, out_grad):
    tokens = queries.shape[0]
    norm = (tokens * lax.axis_size("ctx")) ** (-0.5)
    levels = LOCAL + CROSS
    vmem = pl.BlockSpec(memory_space=pltpu.VMEM)
    scratch = [
        pltpu.VMEM((RING, TOKENS, WIDTH), BF16),
        pltpu.VMEM((RING * RING, 2, CH, WIDTH), BF16),
        pltpu.VMEM((TOKENS, WIDTH), F32),
        pltpu.VMEM((TOKENS, WIDTH), BF16),
        pltpu.VMEM((TOKENS, WIDTH), BF16),
        pltpu.VMEM((RING, TOKENS, WIDTH), BF16),
        pltpu.VMEM((6, TILE, WIDTH), BF16),
        pltpu.VMEM((RING * RING, 2, CH, WIDTH), BF16),
        pltpu.VMEM((RING * RING, CH, WIDTH), BF16),
        pltpu.VMEM((6, 2, CH, WIDTH), BF16),
        pltpu.VMEM((RING, CH, WIDTH), BF16),
        pltpu.VMEM((6, 32, WIDTH), BF16),
        pltpu.VMEM((HEADS, TOKENS, levels), F32),
        pltpu.VMEM((HEADS, TOKENS, CROSS * DH), BF16),
        pltpu.VMEM((HEADS, 3, TILE, TILE), BF16),
        pltpu.VMEM((GROUPS, DH, DH), F32),
        pltpu.VMEM((3, GROUPS, DH, DH), BF16),
        pltpu.VMEM((7, GROUPS, DH, DH), BF16),
        pltpu.VMEM((GROUPS, CROSS * DH, DH), BF16),
        pltpu.VMEM((GROUPS, DH, CROSS * DH), F32),
        pltpu.VMEM((GROUPS, DH, DH), F32),
        pltpu.VMEM((7, GROUPS, DH, DH), BF16),
        pltpu.VMEM((7, GROUPS, DH, DH), BF16),
        pltpu.VMEM((TOKENS, GROUPS * DH), F32),
        pltpu.VMEM((TOKENS, GROUPS * DH), F32),
        pltpu.SemaphoreType.DMA((COPIES,)),
        pltpu.SemaphoreType.DMA((COPIES,)),
    ]
    return pl.pallas_call(
        make_kernel(norm),
        out_shape=(
            jax.ShapeDtypeStruct((TOKENS, WIDTH), BF16),
            jax.ShapeDtypeStruct((TOKENS, WIDTH), BF16),
            jax.ShapeDtypeStruct((TOKENS, GROUPS * DH), BF16),
            jax.ShapeDtypeStruct((TOKENS, GROUPS * DH), BF16),
            jax.ShapeDtypeStruct((CH, WIDTH), F32),
        ),
        in_specs=[vmem] * 7,
        out_specs=(vmem,) * 5,
        scratch_shapes=scratch,
        compiler_params=pltpu.CompilerParams(
            collective_id=0, has_side_effects=True, vmem_limit_bytes=56 << 20
        ),
        name="layer",
    )(
        queries,
        key_heads,
        value_heads,
        class_ids.reshape(1, tokens),
        level_table,
        out_weight,
        out_grad,
    )


def solution(mesh):
    placed = (
        P("ctx", "heads"),
        P("ctx", "heads"),
        P("ctx", "heads"),
        P("ctx"),
        P(None, "heads", None),
        P("ctx", "heads"),
        P("ctx", "heads"),
    )
    return jax.shard_map(
        local,
        mesh=mesh,
        in_specs=placed,
        out_specs=(P("ctx", "heads"),) * 5,
        check_vma=False,
    )
```

profile of v0, /device:TPU:0, one launch (start us, length us, event | category | flops | bytes accessed | tf_op | source)
XLA Modules:
  0.0 67.7 jit_solution(10482565184851322700)
XLA Ops:
  0.6 1.5 %copy.12.tab_ref = f32[64,4,9]{2,1,0:T(4,128)} copy(f32[64,4,9]{0,1,2:T(4,128)} %param.11) | data formatting | bytes 18432 | tf_op args[4]
  2.1 59.9 %layer.1 = (bf16[512,512]{1,0:T(8,128)(2,1)}, bf16[512,512]{1,0:T(8,128)(2,1)}, bf16[512,256]{1,0:T(8,128)(2,1)}, bf16[512,256]{1,0:T(8,128)(2,1)}, f32[64,512]{1,0:T(8,128)}) custom-call(bf16[512,512]{1,0:T(8,128)(2,1)} %q_ref.1, bf16[512,256]{1,0:T(8,128)(2,1)} %k_ref.1, bf16[512,256]{1,0:T(8,128)(2,1)} %v_ref.1, s32[1,512]{1,0:T(1,128)} %bitcast.1, ...), custom_call_target="tpu_custom_call" | custom-call | tf_op jit(solution)/shard_map/layer/pallas_call | solution.py:517
  62.0 0.0 copy-start
  62.0 1.9 %copy.18 = bf16[512,512]{1,0:T(8,128)(2,1)} copy(bf16[512,512]{1,0:T(8,128)(2,1)} %get-tuple-element.10) | data formatting | bytes 1048576
  63.9 0.0 copy-done
  63.9 0.0 copy-start.2
  63.9 0.8 %copy.19 = bf16[512,512]{1,0:T(8,128)(2,1)} copy(bf16[512,512]{1,0:T(8,128)(2,1)S(1)} %copy-done) | data formatting | bytes 1048576
  64.7 0.3 copy-done.2
  65.0 0.0 copy-start.1
  65.0 0.7 %copy.20 = bf16[512,256]{1,0:T(8,128)(2,1)} copy(bf16[512,256]{1,0:T(8,128)(2,1)S(1)} %copy-done.2) | data formatting | bytes 524288
  65.7 0.3 copy-done.1
  66.1 0.0 copy-start.3
  66.1 0.7 %copy.21 = bf16[512,256]{1,0:T(8,128)(2,1)} copy(bf16[512,256]{1,0:T(8,128)(2,1)S(1)} %copy-done.1) | data formatting | bytes 524288
  66.8 0.3 copy-done.3
  67.1 0.7 copy.22
Async XLA Ops:
  62.0 1.9 %copy-start = (bf16[512,512]{1,0:T(8,128)(2,1)S(1)}, bf16[512,512]{1,0:T(8,128)(2,1)}, u32[]{:S(2)}) copy-start(bf16[512,512]{1,0:T(8,128)(2,1)} %get-tuple-element.11) | copy-start | bytes 1572868
  63.9 1.1 %copy-start.2 = (bf16[512,256]{1,0:T(8,128)(2,1)S(1)}, bf16[512,256]{1,0:T(8,128)(2,1)}, u32[]{:S(2)}) copy-start(bf16[512,256]{1,0:T(8,128)(2,1)} %get-tuple-element.12) | copy-start | bytes 786436
  65.0 1.0 %copy-start.1 = (bf16[512,256]{1,0:T(8,128)(2,1)S(1)}, bf16[512,256]{1,0:T(8,128)(2,1)}, u32[]{:S(2)}) copy-start(bf16[512,256]{1,0:T(8,128)(2,1)} %get-tuple-element.13) | copy-start | bytes 786436
  66.1 1.0 %copy-start.3 = (f32[64,512]{1,0:T(8,128)S(1)}, f32[64,512]{1,0:T(8,128)}, u32[]{:S(2)}) copy-start(f32[64,512]{1,0:T(8,128)} %get-tuple-element.14) | copy-start | bytes 393220
where the time goes:
time: 68 us; the launch traced here: 67.7 us
  Pallas kernels  59.9 us (88%)
  local copies, waits for them, and re-layouts  7.21 us (11%)
    pallas_call x1, Pallas kernels, local(): pl.pallas_call(make_kernel(norm), out_shape=(jax.ShapeDtypeStruct((TOKENS...  59.9 us
    unnamed x14, local copies, waits for them, and re-layouts  7.21 us

commit v1 on v0

--- a/solution.py
+++ b/solution.py
@@ -51,11 +51,11 @@
 
 def make_kernel(norm):
     def kernel(
-        q_ref, k_ref, v_ref, ids_ref, tab_ref, w_ref, og_ref,
+        q_hbm, k_hbm, v_hbm, ids_ref, tab_ref, w_hbm, og_hbm,
         proj_ref, dq_ref, dk_ref, dv_ref, wg_ref,
-        ogf, wf, acc, attn, ga, piece, zbuf, wg, wgc, ybuf, xpiece, xbuf,
+        q_ref, k_ref, v_ref, ogf, wf, acc, attn, ga, piece, zbuf, wg, wgc, buf1, half2, buf2,
         scale, wqc, prob, total, ssend, srecv, read, gmat, gacc, gsend, grecv, dka, dva,
-        ssem, rsem,
+        lsem, ssem, rsem,
     ):
         z = lax.axis_index("heads")
         c = lax.axis_index("ctx")
@@ -148,17 +148,35 @@
             pl.semaphore_signal(
                 barrier, inc=1, device_id=device, device_id_type=pl.DeviceIdType.MESH
             )
+
+        fetched = [
+            pltpu.make_async_copy(source, target, lsem.at[i])
+            for i, (source, target) in enumerate(
+                (
+                    (og_hbm, ogf.at[z]),
+                    (w_hbm, wf.at[y, x, core]),
+                    (k_hbm, k_ref),
+                    (v_hbm, v_ref),
+                    (q_hbm, q_ref),
+                )
+            )
+        ]
+        for copy in fetched:
+            copy.start()
+        for copy in fetched:
+            copy.wait()
         pl.semaphore_wait(barrier, len(peers))
 
         def og_half(block, part):
             return ogf.at[block, pl.ds(part * TILE, TILE)]
 
-        ogf[z] = og_ref[...]
         og_copies = gather_start(z_dev, z, og_half)
 
-        own = y * RING + x
-        wf[own, core] = w_ref[...]
-        w_x = [send(wf.at[own, core], wf.at[own, core], x_dev(o)) for o in (1, 3, 2)]
+        left, right = pl.ds(0, TILE), pl.ds(TILE, TILE)
+        mine_l = wf.at[y, x, core, :, left]
+        mine_r = wf.at[y, x, core, :, right]
+        w_one = [send(mine_l, mine_l, x_dev(o)) for o in (1, 3, 2)]
+        w_one += [send(mine_r, mine_r, y_dev(o)) for o in (1, 3, 2)]
 
         for g in range(GROUPS):
             cols = slice(g * DH, (g + 1) * DH)
@@ -166,7 +184,7 @@
         ssend[0] = total[...].astype(BF16)
         s_core = send(ssend.at[0], srecv.at[0], sibling)
 
-        classes = tab_ref.shape[0]
+        classes = tab_ref.shape[2]
         onehot = (
             lax.broadcasted_iota(jnp.int32, (classes, TOKENS), 0) == ids_ref[...]
         ).astype(F32)
@@ -176,19 +194,15 @@
         for number in range(1, levels):
             coef = jnp.where(level == number, coefficient(number), coef)
         for h in range(HEADS):
-            lam = contract(onehot, tab_ref[:, h, :], 0, 0, lax.Precision.HIGHEST)
+            lam = contract(onehot, tab_ref[:, h, :], 0, 1, lax.Precision.HIGHEST)
             scale[h] = lam * coef
 
-        def w_half(block, part):
-            return wf.at[pl.ds(block * RING + part * 2, 2), core]
-
-        def w_row(block):
-            return wf.at[pl.ds(block * RING, RING), core]
-
-        for copy in w_x:
+        for copy in w_one:
             copy.wait_recv()
-        w_y = gather_start(y_dev, y, w_half)
-        w_rows = [send(w_row(y), w_row(y), sibling)]
+        row_l = wf.at[y, :, core, :, left]
+        row_r = wf.at[:, x, core, :, right]
+        w_two_l = [send(row_l, row_l, y_dev(o)) for o in (1, 3, 2)]
+        w_two_r = [send(row_r, row_r, x_dev(o)) for o in (1, 3, 2)]
 
         s_core.wait_recv()
         got = srecv[0].astype(F32)
@@ -270,13 +284,13 @@
             acc[first, cols] = dot(p0, v0)
             acc[second, cols] = dot(p1, v1) + dot(p2, v0)
 
-        lax.fori_loop(0, 2, lambda h, _: (forward(h), 0)[1], 0)
-        w_far = gather_forward(y_dev, y, w_half, w_y)
-        lax.fori_loop(2, HEADS, lambda h, _: (forward(h), 0)[1], 0)
-        w_y[2].wait_recv()
-        w_rows.append(send(w_row(ring(y, -1)), w_row(ring(y, -1)), sibling))
-        w_y[3].wait_recv()
-        w_rows.append(send(w_row(ring(y, 1)), w_row(ring(y, 1)), sibling))
+        lax.fori_loop(0, HEADS, lambda h, _: (forward(h), 0)[1], 0)
+        w_core = []
+        for copies, span in ((w_two_l, left), (w_two_r, right)):
+            for copy in copies:
+                copy.wait_recv()
+            part = wf.at[:, :, core, :, span]
+            w_core.append(send(part, part, sibling))
         exchange(s_y, y, 3, 3)
 
         def across(h):
@@ -284,14 +298,11 @@
             attn[:, cols] = (acc[:, cols] + dot(wqc[h], read[h // 2])).astype(BF16)
 
         lax.fori_loop(0, HEADS, lambda h, _: (across(h), 0)[1], 0)
-        w_far[0].wait_recv()
-        w_far[1].wait_recv()
-        w_rows.append(send(w_row(ring(y, 2)), w_row(ring(y, 2)), sibling))
-        for copy in w_rows:
+        for copy in w_core:
             copy.wait_recv()
 
         def weights(block):
-            return wf[pl.ds(block * RING, RING)].reshape(WIDTH, WIDTH)
+            return wf[block].reshape(WIDTH, WIDTH)
 
         def project(block):
             def step(t, _):
@@ -325,12 +336,11 @@
             def step(t, _):
                 span = pl.ds(pl.multiple_of(t * TILE, TILE), TILE)
                 term = dot_tn(ogf[block, :, span], attn[...]).astype(BF16)
-                wg[pl.ds(block * RING + t * 2, 2)] = term.reshape(2, 2, CH, WIDTH)
+                wg[block, pl.ds(t * 2, 2)] = term.reshape(2, 2, CH, WIDTH)
                 return 0
 
             lax.fori_loop(0, 2, step, 0)
-            span = pl.ds(block * RING, RING)
-            wg_core.append(send(wg.at[span, 1 - core], wgc.at[span], sibling))
+            wg_core.append(send(wg.at[block, :, 1 - core], wgc.at[block], sibling))
 
         back(z, True)
         weight_grad(z)
@@ -345,7 +355,6 @@
         og_far[1].wait_recv()
         back(ring(z, 2), False)
         ga[...] = acc[...].astype(BF16)
-        z_middle = scatter_middle(z_dev, z, z_half, zbuf, z_far)
         weight_grad(ring(z, 2))
 
         def state_grad(g):
@@ -371,16 +380,16 @@
             copy.wait_recv()
 
         def merge(t, _):
-            wgc[t] = (wg[t, core].astype(F32) + wgc[t].astype(F32)).astype(BF16)
+            wgc[t] = (wg[t, :, core].astype(F32) + wgc[t].astype(F32)).astype(BF16)
             return 0
 
-        lax.fori_loop(0, RING * RING, merge, 0)
-
-        def y_half(block, part):
-            return wgc.at[pl.ds(block * RING + part * 2, 2)]
-
-        y_far = scatter_far(y_dev, y, y_half, ybuf)
-        y_near = scatter_near(y_dev, y, y_half, ybuf)
+        lax.fori_loop(0, RING, merge, 0)
+        wg_one_l = [
+            send(wgc.at[ring(y, o), :, :, left], buf1.at[0, o], y_dev(o)) for o in (2, 1, 3)
+        ]
+        wg_one_r = [
+            send(wgc.at[:, ring(x, o), :, right], buf1.at[1, o], x_dev(o)) for o in (2, 1, 3)
+        ]
 
         def backward(g):
             group = pl.ds(pl.multiple_of(g * DH, DH), DH)
@@ -422,8 +431,7 @@
 
         backward_loop = lambda a, b: lax.fori_loop(a, b, lambda g, _: (backward(g), 0)[1], 0)
         backward_loop(0, 1)
-
-        y_middle = scatter_middle(y_dev, y, y_half, ybuf, y_far)
+        z_middle = scatter_middle(z_dev, z, z_half, zbuf, z_far)
         gacc[...] = jnp.zeros_like(gacc)
         for o, copy in zip((1, 2, 3), g_y):
             copy.wait_recv()
@@ -445,15 +453,18 @@
         gsend[0] = (gacc[...] + level_grad(0) * flag(core == 1)).astype(BF16)
         g_core = send(gsend.at[0], grecv.at[0], sibling)
 
-        scatter_wait(y_near, y_middle)
-        xpiece[0:2] = scatter_sum(y, y_half, ybuf, 0).astype(BF16)
-        xpiece[2:4] = scatter_sum(y, y_half, ybuf, 1).astype(BF16)
-
-        def x_half(block, part):
-            return xpiece.at[block, pl.ds(part * 32, 32)]
-
-        x_far = scatter_far(x_dev, x, x_half, xbuf)
-        x_near = scatter_near(x_dev, x, x_half, xbuf)
+        for copies, side, own in (
+            (wg_one_l, 0, wgc[y, :, :, left]),
+            (wg_one_r, 1, wgc[:, x, :, right]),
+        ):
+            for copy in copies:
+                copy.wait_recv()
+            value = own.astype(F32)
+            for o in (1, 2, 3):
+                value += buf1[side, o].astype(F32)
+            half2[side] = value.astype(BF16)
+        wg_two = [send(half2.at[0, ring(x, o)], buf2.at[0, o], x_dev(o)) for o in (2, 1, 3)]
+        wg_two += [send(half2.at[1, ring(y, o)], buf2.at[1, o], y_dev(o)) for o in (2, 1, 3)]
 
         g_core.wait_recv()
         gacc[...] += grecv[0].astype(F32)
@@ -463,10 +474,13 @@
             dk_ref[:, cols] = (dka[:, cols] + dot(v_ref[:, cols], key_side)).astype(BF16)
             dv_ref[:, cols] = (dva[:, cols] + dot_nt(k_ref[:, cols], key_side)).astype(BF16)
 
-        x_middle = scatter_middle(x_dev, x, x_half, xbuf, x_far)
-        scatter_wait(x_near, x_middle)
-        wg_ref[0:32] = scatter_sum(x, x_half, xbuf, 0) * norm
-        wg_ref[32:64] = scatter_sum(x, x_half, xbuf, 1) * norm
+        for copy in wg_two:
+            copy.wait_recv()
+        for side, own, span in ((0, x, left), (1, y, right)):
+            value = half2[side, own].astype(F32)
+            for o in (1, 2, 3):
+                value += buf2[side, o].astype(F32)
+            wg_ref[:, span] = value * norm
 
         scatter_wait(z_near, z_middle)
         proj_ref[0:TILE] = scatter_sum(z, z_half, zbuf, 0).astype(BF16)
@@ -477,7 +491,18 @@
     return kernel
 
 
-COPIES = 60
+COPIES = 64
+
+
+def store(*refs):
+    sem = refs[-1]
+    copies = [
+        pltpu.make_async_copy(refs[i], refs[5 + i], sem.at[i]) for i in range(5)
+    ]
+    for copy in copies:
+        copy.start()
+    for copy in copies:
+        copy.wait()
 
 
 def local(queries, key_heads, value_heads, class_ids, level_table, out_weight, out_grad):
@@ -486,18 +511,21 @@
     levels = LOCAL + CROSS
     vmem = pl.BlockSpec(memory_space=pltpu.VMEM)
     scratch = [
+        pltpu.VMEM((TOKENS, WIDTH), BF16),
+        pltpu.VMEM((TOKENS, GROUPS * DH), BF16),
+        pltpu.VMEM((TOKENS, GROUPS * DH), BF16),
         pltpu.VMEM((RING, TOKENS, WIDTH), BF16),
-        pltpu.VMEM((RING * RING, 2, CH, WIDTH), BF16),
+        pltpu.VMEM((RING, RING, 2, CH, WIDTH), BF16),
         pltpu.VMEM((TOKENS, WIDTH), F32),
         pltpu.VMEM((TOKENS, WIDTH), BF16),
         pltpu.VMEM((TOKENS, WIDTH), BF16),
         pltpu.VMEM((RING, TOKENS, WIDTH), BF16),
         pltpu.VMEM((6, TILE, WIDTH), BF16),
-        pltpu.VMEM((RING * RING, 2, CH, WIDTH), BF16),
-        pltpu.VMEM((RING * RING, CH, WIDTH), BF16),
-        pltpu.VMEM((6, 2, CH, WIDTH), BF16),
-        pltpu.VMEM((RING, CH, WIDTH), BF16),
-        pltpu.VMEM((6, 32, WIDTH), BF16),
+        pltpu.VMEM((RING, RING, 2, CH, WIDTH), BF16),
+        pltpu.VMEM((RING, RING, CH, WIDTH), BF16),
+        pltpu.VMEM((2, RING, RING, CH, TILE), BF16),
+        pltpu.VMEM((2, RING, CH, TILE), BF16),
+        pltpu.VMEM((2, RING, CH, TILE), BF16),
         pltpu.VMEM((HEADS, TOKENS, levels), F32),
         pltpu.VMEM((HEADS, TOKENS, CROSS * DH), BF16),
         pltpu.VMEM((HEADS, 3, TILE, TILE), BF16),
@@ -511,19 +539,22 @@
         pltpu.VMEM((7, GROUPS, DH, DH), BF16),
         pltpu.VMEM((TOKENS, GROUPS * DH), F32),
         pltpu.VMEM((TOKENS, GROUPS * DH), F32),
+        pltpu.SemaphoreType.DMA((5,)),
         pltpu.SemaphoreType.DMA((COPIES,)),
         pltpu.SemaphoreType.DMA((COPIES,)),
     ]
-    return pl.pallas_call(
+    hbm = pl.BlockSpec(memory_space=pl.ANY)
+    shapes = (
+        ((TOKENS, WIDTH), BF16),
+        ((TOKENS, WIDTH), BF16),
+        ((TOKENS, GROUPS * DH), BF16),
+        ((TOKENS, GROUPS * DH), BF16),
+        ((CH, WIDTH), F32),
+    )
+    results = pl.pallas_call(
         make_kernel(norm),
-        out_shape=(
-            jax.ShapeDtypeStruct((TOKENS, WIDTH), BF16),
-            jax.ShapeDtypeStruct((TOKENS, WIDTH), BF16),
-            jax.ShapeDtypeStruct((TOKENS, GROUPS * DH), BF16),
-            jax.ShapeDtypeStruct((TOKENS, GROUPS * DH), BF16),
-            jax.ShapeDtypeStruct((CH, WIDTH), F32),
-        ),
-        in_specs=[vmem] * 7,
+        out_shape=tuple(pltpu.VMEM(*shape) for shape in shapes),
+        in_specs=[hbm, hbm, hbm, vmem, vmem, hbm, hbm],
         out_specs=(vmem,) * 5,
         scratch_shapes=scratch,
         compiler_params=pltpu.CompilerParams(
@@ -535,10 +566,18 @@
         key_heads,
         value_heads,
         class_ids.reshape(1, tokens),
-        level_table,
+        level_table.transpose(2, 1, 0),
         out_weight,
         out_grad,
     )
+    return pl.pallas_call(
+        store,
+        out_shape=tuple(jax.ShapeDtypeStruct(*shape) for shape in shapes),
+        in_specs=[vmem] * 5,
+        out_specs=(pl.BlockSpec(memory_space=pl.ANY),) * 5,
+        scratch_shapes=[pltpu.SemaphoreType.DMA((5,))],
+        name="store",
+    )(*(pltpu.with_memory_space_constraint(result, pltpu.VMEM) for result in results))
 
 
 def solution(mesh):

time: 68 us -> 55.5 us (0.82)
  local copies, waits for them, and re-layouts: 7.21 us -> 0 us
  Pallas kernels: 59.9 us -> 54.7 us
    unnamed x14 -> x0, local copies, waits for them, and re-layouts: 7.21 us -> none
    pallas_call x1 -> x2, Pallas kernels: 59.9 us -> 54.7 us  [the longest x1 53.5 us: local(): pl.pallas_call(make_kernel(norm), out_shape=tuple((pltpu.VMEM(*shape) for...]
where the time goes in v1:
time: 55.5 us; the launch traced here: 55.3 us
  Pallas kernels  54.7 us (99%)
  between operations  0.64 us (1%)
    pallas_call x1, Pallas kernels, local(): pl.pallas_call(make_kernel(norm), out_shape=tuple((pltpu.VMEM(*shape) for...  53.5 us
    pallas_call x1, Pallas kernels, local(): pl.pallas_call(store, out_shape=tuple((jax.ShapeDtypeStruct(*shape) for s...  1.22 us

profile of v1, /device:TPU:0, one launch (start us, length us, event | category | flops | bytes accessed | tf_op | source)
XLA Modules:
  0.0 55.3 jit_solution(3600204892101491333)
XLA Ops:
  0.6 53.5 %layer.1 = (bf16[512,512]{1,0:T(8,128)(2,1)S(1)}, bf16[512,512]{1,0:T(8,128)(2,1)S(1)}, bf16[512,256]{1,0:T(8,128)(2,1)S(1)}, bf16[512,256]{1,0:T(8,128)(2,1)S(1)}, f32[64,512]{1,0:T(8,128)S(1)}) custom-call(bf16[512,512]{1,0:T(8,128)(2,1)} %q_hbm.1, bf16[512,256]{1,0:T(8,128)(2,1)} %k_hbm.1, bf16[512,256]{1,0:T(8,128)(2,1)} %v_hbm.1, s32[1,512]{1,0:T(1,128)} %bitcast.3, ...), custom_call_target="tpu_custom_call" | custom-call | tf_op jit(solution)/shard_map/layer/pallas_call | solution.py:554
  54.1 1.2 %store.1 = (bf16[512,512]{1,0:T(8,128)(2,1)}, bf16[512,512]{1,0:T(8,128)(2,1)}, bf16[512,256]{1,0:T(8,128)(2,1)}, bf16[512,256]{1,0:T(8,128)(2,1)}, f32[64,512]{1,0:T(8,128)}) custom-call(bf16[512,512]{1,0:T(8,128)(2,1)S(1)} %get-tuple-element.10.refs_0_, bf16[512,512]{1,0:T(8,128)(2,1)S(1)} %get-tuple-element.11.refs_1_, ...), custom_call_target="tpu_custom_call" | custom-call | tf_op jit(solution)/shard_map/store/pallas_call | solution.py:573

commit v2 on v1

--- a/solution.py
+++ b/solution.py
@@ -197,13 +197,6 @@
             lam = contract(onehot, tab_ref[:, h, :], 0, 1, lax.Precision.HIGHEST)
             scale[h] = lam * coef
 
-        for copy in w_one:
-            copy.wait_recv()
-        row_l = wf.at[y, :, core, :, left]
-        row_r = wf.at[:, x, core, :, right]
-        w_two_l = [send(row_l, row_l, y_dev(o)) for o in (1, 3, 2)]
-        w_two_r = [send(row_r, row_r, x_dev(o)) for o in (1, 3, 2)]
-
         s_core.wait_recv()
         got = srecv[0].astype(F32)
         for g in range(GROUPS):
@@ -211,6 +204,13 @@
         total[...] += got
         ssend[1] = total[...].astype(BF16)
         s_x = [send(ssend.at[1], srecv.at[o], x_dev(o)) for o in (1, 2, 3)]
+
+        for copy in w_one:
+            copy.wait_recv()
+        row_l = wf.at[y, :, core, :, left]
+        row_r = wf.at[:, x, core, :, right]
+        w_two_l = [send(row_l, row_l, y_dev(o)) for o in (1, 3, 2)]
+        w_two_r = [send(row_r, row_r, x_dev(o)) for o in (1, 3, 2)]
 
         def weigh(h):
             cols = pl.ds(pl.multiple_of(h * DH, DH), DH)
@@ -305,57 +305,35 @@
             return wf[block].reshape(WIDTH, WIDTH)
 
         def project(block):
-            def step(t, _):
-                span = pl.ds(pl.multiple_of(t * TILE, TILE), TILE)
-                piece[block, span] = dot_nt(attn[span], weights(block)).astype(BF16)
-                return 0
-
-            lax.fori_loop(0, 2, step, 0)
+            piece[block] = dot_nt(attn[...], weights(block)).astype(BF16)
 
         def z_half(block, part):
             return piece.at[block, pl.ds(part * TILE, TILE)]
 
+        def back(block):
+            return dot(ogf[block], weights(block))
+
+        wg_core = []
+
+        def weight_grad(block):
+            term = dot_tn(ogf[block], attn[...]).astype(BF16)
+            wg[block] = term.reshape(RING, 2, CH, WIDTH)
+            wg_core.append(send(wg.at[block, :, 1 - core], wgc.at[block], sibling))
+
         project(ring(z, 2))
         z_far = scatter_far(z_dev, z, z_half, zbuf)
+        og_copies[2].wait_recv()
+        og_copies[3].wait_recv()
+        acc[...] = back(z) + back(ring(z, -1)) + back(ring(z, 1))
         project(ring(z, 1))
         project(ring(z, -1))
         z_near = scatter_near(z_dev, z, z_half, zbuf)
-
-        def back(block, start):
-            def step(t, _):
-                span = pl.ds(pl.multiple_of(t * TILE, TILE), TILE)
-                term = dot(ogf[block, span], weights(block))
-                acc[span] = term if start else acc[span] + term
-                return 0
-
-            lax.fori_loop(0, 2, step, 0)
-
-        wg_core = []
-
-        def weight_grad(block):
-            def step(t, _):
-                span = pl.ds(pl.multiple_of(t * TILE, TILE), TILE)
-                term = dot_tn(ogf[block, :, span], attn[...]).astype(BF16)
-                wg[block, pl.ds(t * 2, 2)] = term.reshape(2, 2, CH, WIDTH)
-                return 0
-
-            lax.fori_loop(0, 2, step, 0)
-            wg_core.append(send(wg.at[block, :, 1 - core], wgc.at[block], sibling))
-
-        back(z, True)
         weight_grad(z)
-        project(z)
-        og_copies[2].wait_recv()
-        back(ring(z, -1), False)
-        og_copies[3].wait_recv()
-        back(ring(z, 1), False)
         weight_grad(ring(z, -1))
         weight_grad(ring(z, 1))
         og_far[0].wait_recv()
         og_far[1].wait_recv()
-        back(ring(z, 2), False)
-        ga[...] = acc[...].astype(BF16)
-        weight_grad(ring(z, 2))
+        ga[...] = (acc[...] + back(ring(z, 2))).astype(BF16)
 
         def state_grad(g):
             value = jnp.zeros((DH, CROSS * DH), F32)
@@ -376,6 +354,8 @@
             gsend[o] = (level_grad(3) * same + level_grad(4) * (1.0 - same)).astype(BF16)
             g_y.append(send(gsend.at[o], grecv.at[o], y_dev(o)))
 
+        weight_grad(ring(z, 2))
+        project(z)
         for copy in wg_core:
             copy.wait_recv()
 
@@ -384,6 +364,20 @@
             return 0
 
         lax.fori_loop(0, RING, merge, 0)
+        gacc[...] = jnp.zeros_like(gacc)
+        for o, copy in zip((1, 2, 3), g_y):
+            copy.wait_recv()
+            gacc[...] += grecv[o].astype(F32) * flag(ring(y, -o) > y)
+        g_x = []
+        for o in (1, 2, 3):
+            same = flag(x // 2 == ring(x, o) // 2)
+            lower = flag(x > ring(x, o))
+            gsend[3 + o] = (
+                gacc[...]
+                + level_grad(1) * (lower * same)
+                + level_grad(2) * (lower * (1.0 - same))
+            ).astype(BF16)
+            g_x.append(send(gsend.at[3 + o], grecv.at[3 + o], x_dev(o)))
         wg_one_l = [
             send(wgc.at[ring(y, o), :, :, left], buf1.at[0, o], y_dev(o)) for o in (2, 1, 3)
         ]
@@ -432,20 +426,6 @@
         backward_loop = lambda a, b: lax.fori_loop(a, b, lambda g, _: (backward(g), 0)[1], 0)
         backward_loop(0, 1)
         z_middle = scatter_middle(z_dev, z, z_half, zbuf, z_far)
-        gacc[...] = jnp.zeros_like(gacc)
-        for o, copy in zip((1, 2, 3), g_y):
-            copy.wait_recv()
-            gacc[...] += grecv[o].astype(F32) * flag(ring(y, -o) > y)
-        g_x = []
-        for o in (1, 2, 3):
-            same = flag(x // 2 == ring(x, o) // 2)
-            lower = flag(x > ring(x, o))
-            gsend[3 + o] = (
-                gacc[...]
-                + level_grad(1) * (lower * same)
-                + level_grad(2) * (lower * (1.0 - same))
-            ).astype(BF16)
-            g_x.append(send(gsend.at[3 + o], grecv.at[3 + o], x_dev(o)))
         backward_loop(1, 2)
         for o, copy in zip((1, 2, 3), g_x):
             copy.wait_recv()

time: 55.5 us -> 50.1 us (0.903)
  Pallas kernels: 54.7 us -> 49.3 us
    pallas_call x1, Pallas kernels: 53.5 us -> 48.1 us  [local(): pl.pallas_call(make_kernel(norm), out_shape=tuple((pltpu.VMEM(*shape) for...]
where the time goes in v2:
time: 50.1 us; the launch traced here: 49.9 us
  Pallas kernels  49.3 us (98%)
  between operations  0.64 us (1%)
    pallas_call x1, Pallas kernels, local(): pl.pallas_call(make_kernel(norm), out_shape=tuple((pltpu.VMEM(*shape) for...  48.1 us
    pallas_call x1, Pallas kernels, local(): pl.pallas_call(store, out_shape=tuple((jax.ShapeDtypeStruct(*shape) for s...  1.22 us

profile of v2, /device:TPU:0, one launch (start us, length us, event | category | flops | bytes accessed | tf_op | source)
XLA Modules:
  0.0 49.9 jit_solution(12096901875638770998)
XLA Ops:
  0.6 48.1 %layer.1 = (bf16[512,512]{1,0:T(8,128)(2,1)S(1)}, bf16[512,512]{1,0:T(8,128)(2,1)S(1)}, bf16[512,256]{1,0:T(8,128)(2,1)S(1)}, bf16[512,256]{1,0:T(8,128)(2,1)S(1)}, f32[64,512]{1,0:T(8,128)S(1)}) custom-call(bf16[512,512]{1,0:T(8,128)(2,1)} %q_hbm.1, bf16[512,256]{1,0:T(8,128)(2,1)} %k_hbm.1, bf16[512,256]{1,0:T(8,128)(2,1)} %v_hbm.1, s32[1,512]{1,0:T(1,128)} %bitcast.3, ...), custom_call_target="tpu_custom_call" | custom-call | tf_op jit(solution)/shard_map/layer/pallas_call | solution.py:534
  48.7 1.2 %store.1 = (bf16[512,512]{1,0:T(8,128)(2,1)}, bf16[512,512]{1,0:T(8,128)(2,1)}, bf16[512,256]{1,0:T(8,128)(2,1)}, bf16[512,256]{1,0:T(8,128)(2,1)}, f32[64,512]{1,0:T(8,128)}) custom-call(bf16[512,512]{1,0:T(8,128)(2,1)S(1)} %get-tuple-element.10.refs_0_, bf16[512,512]{1,0:T(8,128)(2,1)S(1)} %get-tuple-element.11.refs_1_, ...), custom_call_target="tpu_custom_call" | custom-call | tf_op jit(solution)/shard_map/store/pallas_call | solution.py:553

commit v3 on v2

--- a/solution.py
+++ b/solution.py
@@ -51,9 +51,9 @@
 
 def make_kernel(norm):
     def kernel(
-        q_hbm, k_hbm, v_hbm, ids_ref, tab_ref, w_hbm, og_hbm,
+        q_hbm, k_hbm, v_hbm, ids_hbm, tab_hbm, w_hbm, og_hbm,
         proj_ref, dq_ref, dk_ref, dv_ref, wg_ref,
-        q_ref, k_ref, v_ref, ogf, wf, acc, attn, ga, piece, zbuf, wg, wgc, buf1, half2, buf2,
+        q_ref, k_ref, v_ref, ids_ref, tab_ref, ogf, wf, acc, attn, ga, piece, zbuf, wg, wgc, buf1, half2, buf2,
         scale, wqc, prob, total, ssend, srecv, read, gmat, gacc, gsend, grecv, dka, dva,
         lsem, ssem, rsem,
     ):
@@ -91,12 +91,12 @@
             sent.append(copy)
             return copy
 
-        def gather_start(dev, index, half):
+        def gather_start(dev, index, source, half):
             right, left = dev(1), dev(-1)
-            a = send(half(index, 0), half(index, 0), right)
-            b = send(half(index, 1), half(index, 1), left)
-            d = send(half(index, 1), half(index, 1), right)
-            e = send(half(index, 0), half(index, 0), left)
+            a = send(source(0), half(index, 0), right)
+            b = send(source(1), half(index, 1), left)
+            d = send(source(1), half(index, 1), right)
+            e = send(source(0), half(index, 0), left)
             return a, b, d, e
 
         def gather_forward(dev, index, half, copies):
@@ -130,16 +130,6 @@
             b = send(before, buf.at[5], dev(-1))
             return a, b
 
-        def scatter_wait(near, middle):
-            for copy in near + middle:
-                copy.wait_recv()
-
-        def scatter_sum(index, half, buf, part):
-            own = half(index, part)[...].astype(F32)
-            if part == 0:
-                return own + buf[2].astype(F32) + buf[4].astype(F32)
-            return own + buf[1].astype(F32) + buf[5].astype(F32)
-
         barrier = pltpu.get_barrier_semaphore()
         peers = [z_dev(1), z_dev(-1), sibling]
         for offset in (1, 2, 3):
@@ -158,32 +148,39 @@
                     (k_hbm, k_ref),
                     (v_hbm, v_ref),
                     (q_hbm, q_ref),
+                    (ids_hbm, ids_ref),
+                    (tab_hbm, tab_ref),
                 )
             )
         ]
         for copy in fetched:
             copy.start()
-        for copy in fetched:
-            copy.wait()
         pl.semaphore_wait(barrier, len(peers))
 
         def og_half(block, part):
             return ogf.at[block, pl.ds(part * TILE, TILE)]
 
-        og_copies = gather_start(z_dev, z, og_half)
+        def og_own(part):
+            return og_hbm.at[pl.ds(part * TILE, TILE)]
+
+        og_copies = gather_start(z_dev, z, og_own, og_half)
 
         left, right = pl.ds(0, TILE), pl.ds(TILE, TILE)
         mine_l = wf.at[y, x, core, :, left]
         mine_r = wf.at[y, x, core, :, right]
-        w_one = [send(mine_l, mine_l, x_dev(o)) for o in (1, 3, 2)]
-        w_one += [send(mine_r, mine_r, y_dev(o)) for o in (1, 3, 2)]
-
+        w_one = [send(w_hbm.at[:, left], mine_l, x_dev(o)) for o in (1, 3, 2)]
+        w_one += [send(w_hbm.at[:, right], mine_r, y_dev(o)) for o in (1, 3, 2)]
+
+        fetched[2].wait()
+        fetched[3].wait()
         for g in range(GROUPS):
             cols = slice(g * DH, (g + 1) * DH)
             total[g] = dot_tn(k_ref[:, cols], v_ref[:, cols])
         ssend[0] = total[...].astype(BF16)
         s_core = send(ssend.at[0], srecv.at[0], sibling)
 
+        for copy in fetched[4:] + fetched[:2]:
+            copy.wait()
         classes = tab_ref.shape[2]
         onehot = (
             lax.broadcasted_iota(jnp.int32, (classes, TOKENS), 0) == ids_ref[...]
@@ -334,6 +331,7 @@
         og_far[0].wait_recv()
         og_far[1].wait_recv()
         ga[...] = (acc[...] + back(ring(z, 2))).astype(BF16)
+        weight_grad(ring(z, 2))
 
         def state_grad(g):
             value = jnp.zeros((DH, CROSS * DH), F32)
@@ -354,8 +352,6 @@
             gsend[o] = (level_grad(3) * same + level_grad(4) * (1.0 - same)).astype(BF16)
             g_y.append(send(gsend.at[o], grecv.at[o], y_dev(o)))
 
-        weight_grad(ring(z, 2))
-        project(z)
         for copy in wg_core:
             copy.wait_recv()
 
@@ -364,6 +360,10 @@
             return 0
 
         lax.fori_loop(0, RING, merge, 0)
+        wg_one_l = [
+            send(wgc.at[ring(y, o), :, :, left], buf1.at[0, o], y_dev(o)) for o in (2, 1, 3)
+        ]
+        project(z)
         gacc[...] = jnp.zeros_like(gacc)
         for o, copy in zip((1, 2, 3), g_y):
             copy.wait_recv()
@@ -378,9 +378,6 @@
                 + level_grad(2) * (lower * (1.0 - same))
             ).astype(BF16)
             g_x.append(send(gsend.at[3 + o], grecv.at[3 + o], x_dev(o)))
-        wg_one_l = [
-            send(wgc.at[ring(y, o), :, :, left], buf1.at[0, o], y_dev(o)) for o in (2, 1, 3)
-        ]
         wg_one_r = [
             send(wgc.at[:, ring(x, o), :, right], buf1.at[1, o], x_dev(o)) for o in (2, 1, 3)
         ]
@@ -424,14 +421,14 @@
                     dva[second, group] += dv1
 
         backward_loop = lambda a, b: lax.fori_loop(a, b, lambda g, _: (backward(g), 0)[1], 0)
+        z_middle = scatter_middle(z_dev, z, z_half, zbuf, z_far)
         backward_loop(0, 1)
-        z_middle = scatter_middle(z_dev, z, z_half, zbuf, z_far)
-        backward_loop(1, 2)
         for o, copy in zip((1, 2, 3), g_x):
             copy.wait_recv()
             gacc[...] += grecv[3 + o].astype(F32)
         gsend[0] = (gacc[...] + level_grad(0) * flag(core == 1)).astype(BF16)
         g_core = send(gsend.at[0], grecv.at[0], sibling)
+        backward_loop(1, 2)
 
         for copies, side, own in (
             (wg_one_l, 0, wgc[y, :, :, left]),
@@ -454,6 +451,10 @@
             dk_ref[:, cols] = (dka[:, cols] + dot(v_ref[:, cols], key_side)).astype(BF16)
             dv_ref[:, cols] = (dva[:, cols] + dot_nt(k_ref[:, cols], key_side)).astype(BF16)
 
+        for copy in z_near:
+            copy.wait_recv()
+        acc[0:TILE] = piece[z, 0:TILE].astype(F32) + zbuf[4].astype(F32)
+        acc[TILE:] = piece[z, TILE:].astype(F32) + zbuf[1].astype(F32)
         for copy in wg_two:
             copy.wait_recv()
         for side, own, span in ((0, x, left), (1, y, right)):
@@ -462,9 +463,10 @@
                 value += buf2[side, o].astype(F32)
             wg_ref[:, span] = value * norm
 
-        scatter_wait(z_near, z_middle)
-        proj_ref[0:TILE] = scatter_sum(z, z_half, zbuf, 0).astype(BF16)
-        proj_ref[TILE:] = scatter_sum(z, z_half, zbuf, 1).astype(BF16)
+        for copy in z_middle:
+            copy.wait_recv()
+        proj_ref[0:TILE] = (acc[0:TILE] + zbuf[2].astype(F32)).astype(BF16)
+        proj_ref[TILE:] = (acc[TILE:] + zbuf[5].astype(F32)).astype(BF16)
         for copy in sent:
             copy.wait_send()
 
@@ -494,6 +496,8 @@
         pltpu.VMEM((TOKENS, WIDTH), BF16),
         pltpu.VMEM((TOKENS, GROUPS * DH), BF16),
         pltpu.VMEM((TOKENS, GROUPS * DH), BF16),
+        pltpu.VMEM((1, TOKENS), jnp.int32),
+        pltpu.VMEM((levels, HEADS, level_table.shape[0]), F32),
         pltpu.VMEM((RING, TOKENS, WIDTH), BF16),
         pltpu.VMEM((RING, RING, 2, CH, WIDTH), BF16),
         pltpu.VMEM((TOKENS, WIDTH), F32),
@@ -519,7 +523,7 @@
         pltpu.VMEM((7, GROUPS, DH, DH), BF16),
         pltpu.VMEM((TOKENS, GROUPS * DH), F32),
         pltpu.VMEM((TOKENS, GROUPS * DH), F32),
-        pltpu.SemaphoreType.DMA((5,)),
+        pltpu.SemaphoreType.DMA((7,)),
         pltpu.SemaphoreType.DMA((COPIES,)),
         pltpu.SemaphoreType.DMA((COPIES,)),
     ]
@@ -534,7 +538,7 @@
     results = pl.pallas_call(
         make_kernel(norm),
         out_shape=tuple(pltpu.VMEM(*shape) for shape in shapes),
-        in_specs=[hbm, hbm, hbm, vmem, vmem, hbm, hbm],
+        in_specs=[hbm] * 7,
         out_specs=(vmem,) * 5,
         scratch_shapes=scratch,
         compiler_params=pltpu.CompilerParams(

time: 50.1 us -> 50.7 us (1.012)
  Pallas kernels: 49.3 us -> 50 us
    pallas_call x1, Pallas kernels: 48.1 us -> 48.8 us  [local(): pl.pallas_call(make_kernel(norm), out_shape=tuple((pltpu.VMEM(*shape) for...]
where the time goes in v3:
time: 50.7 us; the launch traced here: 50.6 us
  Pallas kernels  50 us (99%)
  between operations  0.64 us (1%)
    pallas_call x1, Pallas kernels, local(): pl.pallas_call(make_kernel(norm), out_shape=tuple((pltpu.VMEM(*shape) for...  48.8 us
    pallas_call x1, Pallas kernels, local(): pl.pallas_call(store, out_shape=tuple((jax.ShapeDtypeStruct(*shape) for s...  1.22 us

profile of v3, /device:TPU:0, one launch (start us, length us, event | category | flops | bytes accessed | tf_op | source)
XLA Modules:
  0.0 50.6 jit_solution(12645945210169606576)
XLA Ops:
  0.6 48.8 %layer.1 = (bf16[512,512]{1,0:T(8,128)(2,1)S(1)}, bf16[512,512]{1,0:T(8,128)(2,1)S(1)}, bf16[512,256]{1,0:T(8,128)(2,1)S(1)}, bf16[512,256]{1,0:T(8,128)(2,1)S(1)}, f32[64,512]{1,0:T(8,128)S(1)}) custom-call(bf16[512,512]{1,0:T(8,128)(2,1)} %q_hbm.1, bf16[512,256]{1,0:T(8,128)(2,1)} %k_hbm.1, bf16[512,256]{1,0:T(8,128)(2,1)} %v_hbm.1, s32[1,512]{1,0:T(1,128)} %bitcast.3, ...), custom_call_target="tpu_custom_call" | custom-call | tf_op jit(solution)/shard_map/layer/pallas_call | solution.py:538
  49.4 1.2 %store.1 = (bf16[512,512]{1,0:T(8,128)(2,1)}, bf16[512,512]{1,0:T(8,128)(2,1)}, bf16[512,256]{1,0:T(8,128)(2,1)}, bf16[512,256]{1,0:T(8,128)(2,1)}, f32[64,512]{1,0:T(8,128)}) custom-call(bf16[512,512]{1,0:T(8,128)(2,1)S(1)} %get-tuple-element.10.refs_0_, bf16[512,512]{1,0:T(8,128)(2,1)S(1)} %get-tuple-element.11.refs_1_, ...), custom_call_target="tpu_custom_call" | custom-call | tf_op jit(solution)/shard_map/store/pallas_call | solution.py:557

commit v4 on v2

--- a/solution.py
+++ b/solution.py
@@ -92,12 +92,12 @@
             return copy
 
         def gather_start(dev, index, half):
-            right, left = dev(1), dev(-1)
-            a = send(half(index, 0), half(index, 0), right)
-            b = send(half(index, 1), half(index, 1), left)
-            d = send(half(index, 1), half(index, 1), right)
-            e = send(half(index, 0), half(index, 0), left)
-            return a, b, d, e
+            a = send(half(index, 0), half(index, 0), dev(1))
+            return [a, send(half(index, 1), half(index, 1), dev(-1))]
+
+        def gather_rest(dev, index, half):
+            d = send(half(index, 1), half(index, 1), dev(1))
+            return [d, send(half(index, 0), half(index, 0), dev(-1))]
 
         def gather_forward(dev, index, half, copies):
             before, after = ring(index, -1), ring(index, 1)
@@ -211,6 +211,8 @@
         row_r = wf.at[:, x, core, :, right]
         w_two_l = [send(row_l, row_l, y_dev(o)) for o in (1, 3, 2)]
         w_two_r = [send(row_r, row_r, x_dev(o)) for o in (1, 3, 2)]
+
+        og_copies += gather_rest(z_dev, z, og_half)
 
         def weigh(h):
             cols = pl.ds(pl.multiple_of(h * DH, DH), DH)
@@ -298,20 +300,6 @@
             attn[:, cols] = (acc[:, cols] + dot(wqc[h], read[h // 2])).astype(BF16)
 
         lax.fori_loop(0, HEADS, lambda h, _: (across(h), 0)[1], 0)
-        for copy in w_core:
-            copy.wait_recv()
-
-        def weights(block):
-            return wf[block].reshape(WIDTH, WIDTH)
-
-        def project(block):
-            piece[block] = dot_nt(attn[...], weights(block)).astype(BF16)
-
-        def z_half(block, part):
-            return piece.at[block, pl.ds(part * TILE, TILE)]
-
-        def back(block):
-            return dot(ogf[block], weights(block))
 
         wg_core = []
 
@@ -320,20 +308,46 @@
             wg[block] = term.reshape(RING, 2, CH, WIDTH)
             wg_core.append(send(wg.at[block, :, 1 - core], wgc.at[block], sibling))
 
+        weight_grad(z)
+        og_copies[2].wait_recv()
+        weight_grad(ring(z, -1))
+        og_copies[3].wait_recv()
+        weight_grad(ring(z, 1))
+        for copy in w_core:
+            copy.wait_recv()
+
+        def weights(block):
+            return wf[block].reshape(WIDTH, WIDTH)
+
+        def project(block):
+            piece[block] = dot_nt(attn[...], weights(block)).astype(BF16)
+
+        def z_half(block, part):
+            return piece.at[block, pl.ds(part * TILE, TILE)]
+
+        def back(block):
+            return dot(ogf[block], weights(block))
+
+        wg_one_r = []
+
+        def merge(number, block):
+            wg_core[number].wait_recv()
+            wgc[block] = (wg[block, :, core].astype(F32) + wgc[block].astype(F32)).astype(BF16)
+            for o in (2, 1, 3):
+                wg_one_r.append(
+                    send(wgc.at[block, ring(x, o), :, right], buf1.at[1, o, block], x_dev(o))
+                )
+
         project(ring(z, 2))
         z_far = scatter_far(z_dev, z, z_half, zbuf)
-        og_copies[2].wait_recv()
-        og_copies[3].wait_recv()
         acc[...] = back(z) + back(ring(z, -1)) + back(ring(z, 1))
-        project(ring(z, 1))
-        project(ring(z, -1))
-        z_near = scatter_near(z_dev, z, z_half, zbuf)
-        weight_grad(z)
-        weight_grad(ring(z, -1))
-        weight_grad(ring(z, 1))
+        merge(0, z)
+        merge(1, ring(z, -1))
+        merge(2, ring(z, 1))
         og_far[0].wait_recv()
         og_far[1].wait_recv()
         ga[...] = (acc[...] + back(ring(z, 2))).astype(BF16)
+        weight_grad(ring(z, 2))
 
         def state_grad(g):
             value = jnp.zeros((DH, CROSS * DH), F32)
@@ -354,16 +368,15 @@
             gsend[o] = (level_grad(3) * same + level_grad(4) * (1.0 - same)).astype(BF16)
             g_y.append(send(gsend.at[o], grecv.at[o], y_dev(o)))
 
-        weight_grad(ring(z, 2))
+        project(ring(z, 1))
+        project(ring(z, -1))
+        z_near = scatter_near(z_dev, z, z_half, zbuf)
+
+        merge(3, ring(z, 2))
+        wg_one_l = [
+            send(wgc.at[ring(y, o), :, :, left], buf1.at[0, o], y_dev(o)) for o in (2, 1, 3)
+        ]
         project(z)
-        for copy in wg_core:
-            copy.wait_recv()
-
-        def merge(t, _):
-            wgc[t] = (wg[t, :, core].astype(F32) + wgc[t].astype(F32)).astype(BF16)
-            return 0
-
-        lax.fori_loop(0, RING, merge, 0)
         gacc[...] = jnp.zeros_like(gacc)
         for o, copy in zip((1, 2, 3), g_y):
             copy.wait_recv()
@@ -378,12 +391,6 @@
                 + level_grad(2) * (lower * (1.0 - same))
             ).astype(BF16)
             g_x.append(send(gsend.at[3 + o], grecv.at[3 + o], x_dev(o)))
-        wg_one_l = [
-            send(wgc.at[ring(y, o), :, :, left], buf1.at[0, o], y_dev(o)) for o in (2, 1, 3)
-        ]
-        wg_one_r = [
-            send(wgc.at[:, ring(x, o), :, right], buf1.at[1, o], x_dev(o)) for o in (2, 1, 3)
-        ]
 
         def backward(g):
             group = pl.ds(pl.multiple_of(g * DH, DH), DH)
@@ -471,7 +478,7 @@
     return kernel
 
 
-COPIES = 64
+COPIES = 72
 
 
 def store(*refs):

time: 50.1 us -> 48.2 us (0.962)
  Pallas kernels: 49.3 us -> 47.4 us
    pallas_call x1, Pallas kernels: 48.1 us -> 46.2 us  [local(): pl.pallas_call(make_kernel(norm), out_shape=tuple((pltpu.VMEM(*shape) for...]
where the time goes in v4:
time: 48.2 us; the launch traced here: 48 us
  Pallas kernels  47.4 us (98%)
  between operations  0.64 us (1%)
    pallas_call x1, Pallas kernels, local(): pl.pallas_call(make_kernel(norm), out_shape=tuple((pltpu.VMEM(*shape) for...  46.2 us
    pallas_call x1, Pallas kernels, local(): pl.pallas_call(store, out_shape=tuple((jax.ShapeDtypeStruct(*shape) for s...  1.22 us

profile of v4, /device:TPU:0, one launch (start us, length us, event | category | flops | bytes accessed | tf_op | source)
XLA Modules:
  0.0 48.0 jit_solution(7440431165914776030)
XLA Ops:
  0.6 46.2 %layer.1 = (bf16[512,512]{1,0:T(8,128)(2,1)S(1)}, bf16[512,512]{1,0:T(8,128)(2,1)S(1)}, bf16[512,256]{1,0:T(8,128)(2,1)S(1)}, bf16[512,256]{1,0:T(8,128)(2,1)S(1)}, f32[64,512]{1,0:T(8,128)S(1)}) custom-call(bf16[512,512]{1,0:T(8,128)(2,1)} %q_hbm.1, bf16[512,256]{1,0:T(8,128)(2,1)} %k_hbm.1, bf16[512,256]{1,0:T(8,128)(2,1)} %v_hbm.1, s32[1,512]{1,0:T(1,128)} %bitcast.3, ...), custom_call_target="tpu_custom_call" | custom-call | tf_op jit(solution)/shard_map/layer/pallas_call | solution.py:541
  46.8 1.2 %store.1 = (bf16[512,512]{1,0:T(8,128)(2,1)}, bf16[512,512]{1,0:T(8,128)(2,1)}, bf16[512,256]{1,0:T(8,128)(2,1)}, bf16[512,256]{1,0:T(8,128)(2,1)}, f32[64,512]{1,0:T(8,128)}) custom-call(bf16[512,512]{1,0:T(8,128)(2,1)S(1)} %get-tuple-element.10.refs_0_, bf16[512,512]{1,0:T(8,128)(2,1)S(1)} %get-tuple-element.11.refs_1_, ...), custom_call_target="tpu_custom_call" | custom-call | tf_op jit(solution)/shard_map/store/pallas_call | solution.py:560

commit v5 on v4

--- a/solution.py
+++ b/solution.py
@@ -51,9 +51,9 @@
 
 def make_kernel(norm):
     def kernel(
-        q_hbm, k_hbm, v_hbm, ids_ref, tab_ref, w_hbm, og_hbm,
+        q_hbm, k_hbm, v_hbm, ids_hbm, tab_hbm, w_hbm, og_hbm,
         proj_ref, dq_ref, dk_ref, dv_ref, wg_ref,
-        q_ref, k_ref, v_ref, ogf, wf, acc, attn, ga, piece, zbuf, wg, wgc, buf1, half2, buf2,
+        q_ref, k_ref, v_ref, ids_ref, tab_ref, ogf, wf, acc, attn, ga, piece, zbuf, wg, wgc, buf1, half2, buf2,
         scale, wqc, prob, total, ssend, srecv, read, gmat, gacc, gsend, grecv, dka, dva,
         lsem, ssem, rsem,
     ):
@@ -158,13 +158,15 @@
                     (k_hbm, k_ref),
                     (v_hbm, v_ref),
                     (q_hbm, q_ref),
+                    (ids_hbm, ids_ref),
+                    (tab_hbm, tab_ref),
                 )
             )
         ]
         for copy in fetched:
             copy.start()
-        for copy in fetched:
-            copy.wait()
+        fetched[0].wait()
+        fetched[1].wait()
         pl.semaphore_wait(barrier, len(peers))
 
         def og_half(block, part):
@@ -178,12 +180,16 @@
         w_one = [send(mine_l, mine_l, x_dev(o)) for o in (1, 3, 2)]
         w_one += [send(mine_r, mine_r, y_dev(o)) for o in (1, 3, 2)]
 
+        fetched[2].wait()
+        fetched[3].wait()
         for g in range(GROUPS):
             cols = slice(g * DH, (g + 1) * DH)
             total[g] = dot_tn(k_ref[:, cols], v_ref[:, cols])
         ssend[0] = total[...].astype(BF16)
         s_core = send(ssend.at[0], srecv.at[0], sibling)
 
+        for copy in fetched[4:]:
+            copy.wait()
         classes = tab_ref.shape[2]
         onehot = (
             lax.broadcasted_iota(jnp.int32, (classes, TOKENS), 0) == ids_ref[...]
@@ -501,6 +507,8 @@
         pltpu.VMEM((TOKENS, WIDTH), BF16),
         pltpu.VMEM((TOKENS, GROUPS * DH), BF16),
         pltpu.VMEM((TOKENS, GROUPS * DH), BF16),
+        pltpu.VMEM((1, TOKENS), jnp.int32),
+        pltpu.VMEM((levels, HEADS, level_table.shape[0]), F32),
         pltpu.VMEM((RING, TOKENS, WIDTH), BF16),
         pltpu.VMEM((RING, RING, 2, CH, WIDTH), BF16),
         pltpu.VMEM((TOKENS, WIDTH), F32),
@@ -526,7 +534,7 @@
         pltpu.VMEM((7, GROUPS, DH, DH), BF16),
         pltpu.VMEM((TOKENS, GROUPS * DH), F32),
         pltpu.VMEM((TOKENS, GROUPS * DH), F32),
-        pltpu.SemaphoreType.DMA((5,)),
+        pltpu.SemaphoreType.DMA((7,)),
         pltpu.SemaphoreType.DMA((COPIES,)),
         pltpu.SemaphoreType.DMA((COPIES,)),
     ]
@@ -541,7 +549,7 @@
     results = pl.pallas_call(
         make_kernel(norm),
         out_shape=tuple(pltpu.VMEM(*shape) for shape in shapes),
-        in_specs=[hbm, hbm, hbm, vmem, vmem, hbm, hbm],
+        in_specs=[hbm] * 7,
         out_specs=(vmem,) * 5,
         scratch_shapes=scratch,
         compiler_params=pltpu.CompilerParams(

time: 48.2 us -> 47.6 us (0.988)
  Pallas kernels: 47.4 us -> 46.8 us
    pallas_call x1, Pallas kernels: 46.2 us -> 45.6 us  [local(): pl.pallas_call(make_kernel(norm), out_shape=tuple((pltpu.VMEM(*shape) for...]
where the time goes in v5:
time: 47.6 us; the launch traced here: 47.4 us
  Pallas kernels  46.8 us (98%)
  between operations  0.64 us (1%)
    pallas_call x1, Pallas kernels, local(): pl.pallas_call(make_kernel(norm), out_shape=tuple((pltpu.VMEM(*shape) for...  45.6 us
    pallas_call x1, Pallas kernels, local(): pl.pallas_call(store, out_shape=tuple((jax.ShapeDtypeStruct(*shape) for s...  1.22 us

profile of v5, /device:TPU:0, one launch (start us, length us, event | category | flops | bytes accessed | tf_op | source)
XLA Modules:
  0.0 47.4 jit_solution(17759190389353194656)
XLA Ops:
  0.6 45.6 %layer.1 = (bf16[512,512]{1,0:T(8,128)(2,1)S(1)}, bf16[512,512]{1,0:T(8,128)(2,1)S(1)}, bf16[512,256]{1,0:T(8,128)(2,1)S(1)}, bf16[512,256]{1,0:T(8,128)(2,1)S(1)}, f32[64,512]{1,0:T(8,128)S(1)}) custom-call(bf16[512,512]{1,0:T(8,128)(2,1)} %q_hbm.1, bf16[512,256]{1,0:T(8,128)(2,1)} %k_hbm.1, bf16[512,256]{1,0:T(8,128)(2,1)} %v_hbm.1, s32[1,512]{1,0:T(1,128)} %bitcast.3, ...), custom_call_target="tpu_custom_call" | custom-call | tf_op jit(solution)/shard_map/layer/pallas_call | solution.py:549
  46.2 1.2 %store.1 = (bf16[512,512]{1,0:T(8,128)(2,1)}, bf16[512,512]{1,0:T(8,128)(2,1)}, bf16[512,256]{1,0:T(8,128)(2,1)}, bf16[512,256]{1,0:T(8,128)(2,1)}, f32[64,512]{1,0:T(8,128)}) custom-call(bf16[512,512]{1,0:T(8,128)(2,1)S(1)} %get-tuple-element.10.refs_0_, bf16[512,512]{1,0:T(8,128)(2,1)S(1)} %get-tuple-element.11.refs_1_, ...), custom_call_target="tpu_custom_call" | custom-call | tf_op jit(solution)/shard_map/store/pallas_call | solution.py:568
